TPU v7x, 32 devices: a whole 2x2x4 slice. The times are simulated.
32 devices in a mesh: gx: 8 (over y, x, core), sp: 4 (over z).
Axes of the slice: x: 2, y: 2, z: 4, core: 2. Of those that a mesh axis runs over, the one named last changes fastest.
Arguments:
- previous_head: float32 [8, 64, 512], P(None, 'gx', 'sp'), may hold values from -6 to 6
- recharge: float32 [8, 64, 512], P(None, 'gx', 'sp'), may hold values from -6 to 6
- soil_zone: int32 [8, 64, 512], P(None, 'gx', 'sp'), may hold values from 0 to 7
- soil_cond: float32 [8], replicated, may hold values from 0.1 to 1
- soil_store: float32 [8], replicated, may hold values from 0.05 to 0.5
- species: float32 [12, 8, 64, 512], P('sp', None, 'gx'), may hold values from -6 to 6
- mineral_zone: int32 [8, 64, 512], P(None, 'gx', 'sp'), may hold values from 0 to 5
- rate_table: float32 [6, 8], replicated, may hold values from 0.3 to 3
- stoich: float32 [12, 8], replicated, may hold values from -3 to 3
- log_equil: float32 [8], replicated, may hold values from -1 to 1
Outputs:
- head_field: float32 [8, 64, 512], P(None, 'gx', 'sp')
- species_out: float32 [12, 8, 64, 512], P('sp', None, 'gx')
Inputs may be any that keep to these rules, and one draw needn't show every extreme that they name: `soil_zone`: a soil class of 8. `mineral_zone`: a mineral zone class of 6.
All inputs are finite; a program needn't handle non-finite values.
Results may differ from a plain program's by a relative error of at most 0.0003.
Values sent between devices are 32-bit elements; how exact they have to be, the bound alone decides.
No kernel may reach another device: no remote copies, remote signals or barrier semaphores. Data moves between devices by JAX's collectives and lax.ppermute only.
A program may use at most 64 MiB of HBM per device.

v0:
```python
import functools

import jax
import jax.numpy as jnp
from jax import lax
from jax.experimental import pallas as pl
from jax.experimental.pallas import tpu as pltpu
from jax.sharding import PartitionSpec as P


ITERS = 6
NEWTON = 2

time_step = 0.05
dispersion = 0.5
reaction_span = 0.5
newton_damping = 0.5

LANES = 128
VMEM_BYTES = 16 * 1024 * 1024
WHOLE_VMEM_BYTES = 60 * 1024 * 1024
BASIS = ITERS + 1
HALO = ITERS + 1
LAYERS_TOGETHER = 4
PAIRS = [(i, j) for j in range(BASIS) for i in range(j + 1)]
PAIR_AT = {pair: at for at, pair in enumerate(PAIRS)}
PAIR_ROWS = -(-len(PAIRS) // 8) * 8


def harmonic(center, other):
    return 2.0 * center * other / jnp.maximum(center + other, 1e-30)


def pick(labels, table, first):
    value = jnp.zeros(labels.shape, jnp.float32)
    for level in range(table.shape[0]):
        value = jnp.where(labels == level + first, table[level], value)
    return value


def lane_ids(shape):
    return lax.broadcasted_iota(jnp.int32, shape, len(shape) - 1)


def fetch(pairs, sems, later):
    copies = [
        pltpu.make_async_copy(source, target, sems.at[at]) for at, (source, target) in enumerate(pairs + later)
    ]
    for copy in copies:
        copy.start()
    for copy in copies[: len(pairs)]:
        copy.wait()
    return copies[len(pairs) :]


def field_kernel(cond_h, store_h, previous_h, recharge_h, zone_h, species_h, field, sides, *refs):
    *blocks, cond_t, store_t, previous, recharge, zone, species, sems = refs
    (species_copy,) = fetch(
        [(cond_h, cond_t), (store_h, store_t), (previous_h, previous), (recharge_h, recharge), (zone_h, zone)],
        sems,
        [(species_h, species)],
    )
    count = lax.axis_size("sp")
    me = lax.axis_index("sp")
    layers = previous.shape[0]
    shape = previous.shape[1:]
    lane = lane_ids(shape)
    conduct, bound = [], []
    to_left = to_right = jnp.zeros(shape, jnp.float32)
    for z in range(layers):
        labels = zone[z]
        conduct.append(pick(labels, cond_t, 0))
        storage = pick(labels, store_t, 0)
        bound.append(storage)
        values = (storage * previous[z] + recharge[z], (labels + 1).astype(jnp.float32))
        for part, value in enumerate(values):
            at = part * layers + z
            field[at] = value
            here = jnp.logical_and(lane >= at * HALO, lane < (at + 1) * HALO)
            to_left = jnp.where(here, pltpu.roll(value, at * HALO, 1), to_left)
            to_right = jnp.where(here, pltpu.roll(value, (at + 1) * HALO % LANES, 1), to_right)
    power = jnp.zeros(shape, jnp.float32)
    upright = [harmonic(conduct[z], conduct[(z + 1) % layers]) for z in range(layers)]
    for z in range(layers):
        here = conduct[z]
        total = upright[z] + upright[z - 1]
        for axis in range(2):
            face = harmonic(here, pltpu.roll(here, 1, axis))
            total = total + face + pltpu.roll(face, shape[axis] - 1, axis)
        square = bound[z] + 2.0 * total
        square = square * square
        power = power + square * square
    column = jnp.sum(power, axis=0, keepdims=True) * (1.0 / (layers * shape[0]))
    top = jnp.broadcast_to(jnp.max(column, axis=1, keepdims=True), shape)
    for s in range(count):
        tile = jnp.where(me + 1 == s, to_right, jnp.where(me - 1 == s, to_left, 0.0))
        tile = jnp.where(lane >= 2 * layers * HALO, top, tile)
        for g in range(sides.shape[0] // count):
            sides[g * count + s] = tile
    species_copy.wait()
    pack(species, *blocks)


def pack(species, *blocks):
    count = len(blocks)
    me = lax.axis_index("sp")
    groups, layers, rows = species.shape[:3]
    shape = (rows, LANES)
    lane = lane_ids(shape)
    for d in range(count):
        here = jnp.bitwise_xor(me, d)
        sides = (lax.rem(here + count - 1, count), here, lax.rem(here + 1, count))
        at = [pl.ds(pl.multiple_of(i * LANES, LANES), LANES) for i in sides]
        edge = jnp.zeros(shape, jnp.float32)
        for c in range(groups):
            for z in range(layers):
                j = c * layers + z
                blocks[d][j] = species[c, z, :, at[1]]
                edge = jnp.where(lane == 2 * j, pltpu.roll(species[c, z, :, at[2]], 2 * j, 1), edge)
                edge = jnp.where(
                    lane == 2 * j + 1, pltpu.roll(species[c, z, :, at[0]], 2 * j + 2, 1), edge
                )
        blocks[d][groups * layers] = edge


def rim_kernel(groups, *refs):
    *blocks, _, up, down = refs
    rows = blocks[0].shape[1]
    layers = (blocks[0].shape[0] - 1) // groups
    for d, block in enumerate(blocks):
        for c in range(groups):
            at = pl.ds(c * layers, layers)
            up[d * groups + c] = block[at, 0, :]
            down[d * groups + c] = block[at, rows - 1, :]


def rates_kernel(rate_t, mineral, half_rates):
    layers = mineral.shape[0]
    for z in range(layers):
        labels = mineral[z]
        masks = [labels == level for level in range(rate_t.shape[0])]
        for m in range(rate_t.shape[1]):
            rate = jnp.zeros(labels.shape, jnp.float32)
            for level, mask in enumerate(masks):
                rate = jnp.where(mask, reaction_span * rate_t[level, m], rate)
            half_rates[m * layers + z] = rate


def powers_kernel(stoich, powers, products):
    values = stoich[...]
    result = lax.dot_general(
        values,
        values,
        (((0,), (0,)), ((), ())),
        precision=lax.Precision.HIGHEST,
        preferred_element_type=jnp.float32,
    )
    powers[...] = result
    products[...] = result[:, :1] * result[:1, :]


def krylov_kernel(cond_t, store_t, sides, previous, recharge, zone, above, below, basis, kx, ky, kz, scale, sums, cond_s, store_s, pair_s):
    tall_count, count = lax.axis_size("gx"), lax.axis_size("sp")
    me, me_s = lax.axis_index("gx"), lax.axis_index("sp")
    layers, tall, wide = cond_s.shape
    rows = tall // 3
    lane = lane_ids((rows, LANES))
    tops = jnp.max(sides[...], axis=0)
    tops = jnp.max(jnp.where(lane >= 2 * layers * HALO, tops, 0.0), axis=0, keepdims=True)
    top = jnp.sqrt(jnp.sqrt(jnp.max(tops, axis=1, keepdims=True)))
    scale[...] = jnp.broadcast_to(4.0 / top, scale.shape)
    twice = jnp.broadcast_to(2.0 / top, (1, wide))
    fourth = jnp.broadcast_to(4.0 / top, (1, wide))

    for part, block in enumerate((above, None, below)):
        there = me + part - 1
        valid = jnp.logical_and(there >= 0, there < tall_count)
        there = jnp.clip(there, 0, tall_count - 1) * count
        keep = valid.astype(jnp.float32)
        keep_left = jnp.logical_and(valid, me_s > 0).astype(jnp.float32)
        keep_right = jnp.logical_and(valid, me_s < count - 1).astype(jnp.float32)
        left = sides[there + jnp.maximum(me_s - 1, 0)] * keep_left
        right = sides[there + jnp.minimum(me_s + 1, count - 1)] * keep_right
        at = slice(part * rows, (part + 1) * rows)
        for z in range(layers):
            near = []
            for j in (z, layers + z):
                value = jnp.where(lane < HALO, pltpu.roll(right, (LANES - j * HALO) % LANES, 1), 0.0)
                value = jnp.where(
                    lane >= LANES - HALO, pltpu.roll(left, LANES - (j + 1) * HALO, 1), value
                )
                near.append(value)
            if block is None:
                field, labels = None, zone[z] + 1
            else:
                field, labels = block[z] * keep, block[layers + z] * keep
            for half, (field, labels) in enumerate(((field, labels), near)):
                cols = slice(half * LANES, (half + 1) * LANES)
                storage = pick(labels, store_t, 1)
                if field is None:
                    field = storage * previous[z] + recharge[z]
                basis[0, z, at, cols] = field
                cond_s[z, at, cols] = pick(labels, cond_t, 1)
                store_s[z, at, cols] = storage
    kz[0] = jnp.zeros((tall, wide), jnp.float32)
    for z in range(layers):
        here = cond_s[z]
        kx[z] = harmonic(here, pltpu.roll(here, tall - 1, 0))
        ky[z] = harmonic(here, pltpu.roll(here, wide - 1, 1))
        if z + 1 < layers:
            kz[z + 1] = harmonic(here, cond_s[z + 1])

    def operate(k):
        flow = None
        for z in range(layers):
            value = basis[k, z]
            along_x = kx[z] * (value - pltpu.roll(value, tall - 1, 0))
            along_y = ky[z] * (value - pltpu.roll(value, wide - 1, 1))
            image = store_s[z] * value
            image = image + (along_x - pltpu.roll(along_x, 1, 0))
            image = image + (along_y - pltpu.roll(along_y, 1, 1))
            if z + 1 < layers:
                along_z = kz[z + 1] * (value - basis[k, z + 1])
                image = image + along_z
            if z:
                image = image - flow
            flow = along_z
            yield z, value, image

    for z, value, image in operate(0):
        basis[1, z] = image * twice - value

    def step(k, carry):
        for z, value, image in operate(k):
            basis[k + 1, z] = image * fourth - 2.0 * value - basis[k - 1, z]
        return carry

    lax.fori_loop(1, ITERS, step, 0)

    totals = [None] * len(PAIRS)
    for z in range(layers):
        values = [basis[k, z, rows : 2 * rows, :LANES] for k in range(BASIS)]
        for at, (i, j) in enumerate(PAIRS):
            term = values[i] * values[j]
            totals[at] = term if z == 0 else totals[at] + term
    pair_s[...] = jnp.zeros(pair_s.shape, jnp.float32)
    for at, total in enumerate(totals):
        pair_s[at : at + 1, :] = jnp.sum(total, axis=0, keepdims=True)
    full = jnp.sum(pair_s[...], axis=1, keepdims=True)
    lane = lane_ids(pair_s.shape)
    row = lax.broadcasted_iota(jnp.int32, pair_s.shape, 0)
    line = jnp.sum(jnp.where(lane == row, full, 0.0), axis=0, keepdims=True)
    sums[...] = jnp.broadcast_to(line, sums.shape)


def galerkin_weights(gram):
    def inner(i, j):
        return gram[PAIR_AT[(min(i, j), max(i, j))]]

    matrix = {}
    for i in range(ITERS):
        for j in range(i + 1):
            if j == 0:
                matrix[(i, j)] = 2.0 * (inner(i, 0) + inner(i, 1))
            else:
                matrix[(i, j)] = inner(i, j + 1) + inner(i, j - 1) + 2.0 * inner(i, j)
    least = [matrix[(i, i)] * 2e-7 for i in range(ITERS)]
    right = [inner(i, 0) for i in range(ITERS)]
    inverse = []
    for j in range(ITERS):
        pivot = matrix[(j, j)]
        good = pivot > least[j]
        inverse.append(jnp.where(good, 1.0 / jnp.where(good, pivot, 1.0), 0.0))
        for i in range(j + 1, ITERS):
            factor = matrix[(i, j)] * inverse[j]
            right[i] = right[i] - factor * right[j]
            for k in range(j + 1, i + 1):
                matrix[(i, k)] = matrix[(i, k)] - factor * matrix[(k, j)]
    for i in reversed(range(ITERS)):
        for k in range(i + 1, ITERS):
            right[i] = right[i] - matrix[(k, i)] * right[k]
        right[i] = right[i] * inverse[i]
    return right


def react(moved, half_rates, powers, products, stoich, rows, log_equil):
    minerals = len(half_rates)
    first = []
    for m in range(minerals):
        total = None
        for value, row in zip(moved, rows):
            term = stoich[row, m] * value
            total = term if total is None else total + term
        first.append(total - log_equil[m])
    shift = None
    for newton_pass in range(NEWTON):
        affinity = first
        if shift is not None:
            affinity = [value - newton_damping * past for value, past in zip(first, image)]
        tangent = [jnp.tanh(value) for value in affinity]
        gap = [rate * value for rate, value in zip(half_rates, tangent)]
        if shift is not None:
            gap = [value - past for value, past in zip(gap, shift)]
        weight = [rate * (1.0 - value * value) for rate, value in zip(half_rates, tangent)]
        matrix = {(i, j): powers[i, j] for i in range(minerals) for j in range(i + 1)}
        inverse, ahead, drawn = [], [], [None] * minerals
        for k in range(minerals):
            scaled = 1.0 / (1.0 + weight[k] * matrix[(k, k)])
            inverse.append(scaled)
            left = gap[k] if k == 0 else gap[k] - weight[k] * drawn[k]
            ahead.append(left * scaled)
            factor = weight[k] * scaled
            for i in range(k + 1, minerals):
                term = matrix[(i, k)] * ahead[k]
                drawn[i] = term if k == 0 else drawn[i] + term
            for i in range(k + 1, minerals):
                if k == 0:
                    for j in range(1, i + 1):
                        matrix[(i, j)] = powers[i, j] - products[i, j] * factor
                else:
                    part = matrix[(i, k)] * factor
                    for j in range(k + 1, i + 1):
                        matrix[(i, j)] = matrix[(i, j)] - part * matrix[(j, k)]
        step, image = [None] * minerals, [None] * minerals
        for k in reversed(range(minerals)):
            total = None
            for j in range(k + 1, minerals):
                term = matrix[(j, k)] * step[j]
                total = term if total is None else total + term
            step[k] = ahead[k] if total is None else ahead[k] - weight[k] * inverse[k] * total
            if newton_pass + 1 < NEWTON:
                parts = [part for part in (drawn[k], total) if part is not None]
                image[k] = sum(parts, matrix[(k, k)] * step[k])
        delta = [newton_damping * value for value in step]
        shift = delta if shift is None else [past + value for past, value in zip(shift, delta)]
    result = []
    for value, row in zip(moved, rows):
        for m in range(minerals):
            value = value - stoich[row, m] * shift[m]
        result.append(value)
    return result


def finish_kernel(groups, stoich, powers, products, log_equil, scale, sums, half_rates, basis, kx, ky, kz, above, below, *refs):
    count = lax.axis_size("sp")
    blocks, (head_out, *outs, head_s, pair_s) = refs[:count], refs[count:]
    me = lax.axis_index("sp")
    layers, rows = head_out.shape[:2]
    tall, wide = head_s.shape[1:]

    total = jnp.sum(sums[...], axis=0, keepdims=True)
    lane = lane_ids(pair_s.shape)
    row = lax.broadcasted_iota(jnp.int32, pair_s.shape, 0)
    spread = jnp.sum(jnp.where(lane == row, total, 0.0), axis=1, keepdims=True)
    pair_s[...] = jnp.broadcast_to(spread, pair_s.shape)
    gram = [pair_s[at : at + 1, :] for at in range(len(PAIRS))]
    weights = [weight * scale[0:1, :] for weight in galerkin_weights(gram)]
    weights = [jnp.concatenate([weight] * (wide // LANES), axis=1) for weight in weights]
    for z in range(layers):
        value = weights[0] * basis[0, z]
        for k in range(1, ITERS):
            value = value + weights[k] * basis[k, z]
        head_s[z] = value
        head_out[z] = value[rows : 2 * rows, :LANES]

    together = LAYERS_TOGETHER
    shape = (together, rows, LANES)
    lane = lane_ids(shape)
    row = lax.broadcasted_iota(jnp.int32, shape, 1)
    center = slice(rows, 2 * rows)

    def layer(step, carry):
        z = step * together
        here_at = pl.ds(z, together)
        before, after = jnp.maximum(z - 1, 0), jnp.minimum(z + together, layers - 1)

        def beside(ref, base, here):
            first, last = ref[pl.ds(base + before, 1)], ref[pl.ds(base + after, 1)]
            return jnp.concatenate([here[1:], last], axis=0), jnp.concatenate([first, here[:-1]], axis=0)

        value = head_s[here_at, :, :LANES]
        face = kx[here_at, :, :LANES]
        flow = face * (value - pltpu.roll(value, tall - 1, 1))
        faces = [(face[:, center], flow[:, center])]
        faces.append((pltpu.roll(face, 1, 1)[:, center], -pltpu.roll(flow, 1, 1)[:, center]))
        value = head_s[here_at, center, :]
        face = ky[here_at, center, :]
        flow = face * (value - pltpu.roll(value, wide - 1, 2))
        faces.append((face[:, :, :LANES], flow[:, :, :LANES]))
        faces.append((pltpu.roll(face, 1, 2)[:, :, :LANES], -pltpu.roll(flow, 1, 2)[:, :, :LANES]))
        value = value[:, :, :LANES]
        heads = beside(head_s.at[:, center, :LANES], 0, value)
        for shift, other in zip((1, 0), heads):
            face = kz[pl.ds(z + shift, together), center, :LANES]
            faces.append((face, face * (value - other)))
        outward = None
        inward = []
        for face, flow in faces:
            term = jnp.maximum(flow, 0.0) + dispersion * face
            outward = term if outward is None else outward + term
            inward.append(time_step * (dispersion * face - jnp.minimum(flow, 0.0)))
        stay = 1.0 - time_step * outward

        moved, table_rows = [], []
        for d, block in enumerate(blocks):
            group = jnp.bitwise_xor(me, d)
            edge = block[groups * layers]
            for c in range(groups):
                at = c * layers
                here = block[pl.ds(at + z, together)]
                side = jnp.stack([pltpu.roll(edge, LANES - 1 - 2 * (at + z + u), 1) for u in range(together)])
                edge_at = d * groups + c
                lines = [ref[edge_at, here_at, :][:, None, :] for ref in (below, above)]
                following = jnp.where(row == rows - 1, lines[0], pltpu.roll(here, rows - 1, 1))
                preceding = jnp.where(row == 0, lines[1], pltpu.roll(here, 1, 1))
                result = stay * here + inward[0] * following + inward[1] * preceding
                result = result + inward[2] * jnp.where(lane == LANES - 1, side, pltpu.roll(here, LANES - 1, 2))
                result = result + inward[3] * jnp.where(lane == 0, side, pltpu.roll(here, 1, 2))
                over, under = beside(block, at, here)
                moved.append(result + inward[4] * over + inward[5] * under)
                table_rows.append(group * groups + c)
        rates = [half_rates[pl.ds(m * layers + z, together)] for m in range(half_rates.shape[0] // layers)]
        reacted = react(moved, rates, powers, products, stoich, table_rows, log_equil)
        for at, result in enumerate(reacted):
            outs[at // groups][pl.ds((at % groups) * layers + z, together)] = result
        return carry

    lax.fori_loop(0, layers // together, layer, 0)


def place_kernel(*refs):
    *blocks, out = refs
    me = lax.axis_index("sp")
    groups, layers = out.shape[:2]
    for d, block in enumerate(blocks):
        column = pl.multiple_of(jnp.bitwise_xor(me, d) * LANES, LANES)
        for c in range(groups):
            for z in range(layers):
                out[c, z, :, pl.ds(column, LANES)] = block[c * layers + z]


def call(kernel, tables, arrays, out_shapes, scratch=(), space=pltpu.VMEM, limit=VMEM_BYTES):
    smem = pl.BlockSpec(memory_space=pltpu.SMEM)
    vmem = pl.BlockSpec(memory_space=pltpu.VMEM)
    outside = pl.BlockSpec(memory_space=space)
    shapes = [jax.ShapeDtypeStruct(shape, jnp.float32) for shape in out_shapes]
    return pl.pallas_call(
        kernel,
        out_shape=shapes,
        in_specs=[smem] * len(tables) + [outside] * len(arrays),
        out_specs=[vmem] * len(shapes),
        scratch_shapes=[pltpu.VMEM(one, jnp.float32) if isinstance(one, tuple) else one for one in scratch],
        compiler_params=pltpu.CompilerParams(vmem_limit_bytes=limit),
        cost_estimate=pl.CostEstimate(flops=200_000_000, bytes_accessed=4_000_000, transcendentals=0),
    )(*tables, *arrays)


def shifted(array, axis, amount):
    count = lax.axis_size(axis)
    return lax.ppermute(array, axis, [(i, (i + amount) % count) for i in range(count)])


def swapped(array, axis, mask):
    count = lax.axis_size(axis)
    return lax.ppermute(array, axis, [(i, i ^ mask) for i in range(count)])


def per_device(
    previous_head,
    recharge,
    soil_zone,
    soil_cond,
    soil_store,
    species,
    mineral_zone,
    rate_table,
    stoich,
    log_equil,
):
    count = lax.axis_size("sp")
    devices = count * lax.axis_size("gx")
    layers, rows, columns = previous_head.shape
    groups = species.shape[0]
    assert columns == LANES and layers == 8 and rows == 8 and count & (count - 1) == 0
    assert 2 * layers * HALO < LANES and 2 * groups * layers <= LANES
    tile = (rows, LANES)
    everywhere = ("gx", "sp")

    field, sides, *blocks = call(
        field_kernel,
        [],
        [soil_cond, soil_store, previous_head, recharge, soil_zone, species],
        [(2 * layers,) + tile, (devices,) + tile] + [(groups * layers + 1,) + tile] * count,
        [pltpu.SMEM(soil_cond.shape, jnp.float32), pltpu.SMEM(soil_store.shape, jnp.float32)]
        + [(layers,) + tile] * 2
        + [pltpu.VMEM((layers,) + tile, jnp.int32), species.shape, pltpu.SemaphoreType.DMA((6,))],
        pltpu.HBM,
        WHOLE_VMEM_BYTES,
    )
    sides = lax.all_to_all(sides, everywhere, 0, 0, tiled=True)
    below = shifted(field, "gx", -1)
    above = shifted(field, "gx", 1)
    arrived = {}
    for d in range(count - 1, 0, -1):
        arrived[d] = swapped(blocks[d], "sp", d)
    blocks = [blocks[0]] + [arrived[d] for d in range(1, count)]
    powers, products = call(powers_kernel, [], [stoich], [(stoich.shape[1],) * 2] * 2)
    extended = (layers, 3 * rows, 2 * LANES)
    basis, kx, ky, kz, scale, sums = call(
        krylov_kernel,
        [soil_cond, soil_store],
        [sides, previous_head, recharge, soil_zone, above, below],
        [(BASIS,) + extended, extended, extended, (layers + 1,) + extended[1:], tile, (devices, LANES)],
        [extended, extended, (PAIR_ROWS, LANES)],
    )
    sums = lax.all_to_all(sums, everywhere, 0, 0, tiled=True)
    rims = call(
        functools.partial(rim_kernel, groups), [], blocks + [scale], [(count * groups, layers, LANES)] * 2
    )
    below, above = shifted(rims[0], "gx", -1), shifted(rims[1], "gx", 1)
    (half_rates,) = call(rates_kernel, [rate_table], [mineral_zone], [(rate_table.shape[1] * layers,) + tile])
    head_field, *reacted = call(
        functools.partial(finish_kernel, groups),
        [stoich, powers, products, log_equil],
        [scale, sums, half_rates, basis, kx, ky, kz, above, below] + blocks,
        [(layers,) + tile] + [(groups * layers,) + tile] * count,
        [extended, (PAIR_ROWS, LANES)],
    )
    arrived = {d: swapped(reacted[d], "sp", d) for d in range(count - 1, 0, -1)}
    (species_out,) = call(place_kernel, [], [reacted[0]] + [arrived[d] for d in range(1, count)], [species.shape])
    return (head_field, species_out)


def solution(mesh):
    in_specs = (
        P(None, "gx", "sp"),
        P(None, "gx", "sp"),
        P(None, "gx", "sp"),
        P(),
        P(),
        P("sp", None, "gx", None),
        P(None, "gx", "sp"),
        P(),
        P(),
        P(),
    )
    out_specs = (P(None, "gx", "sp"), P("sp", None, "gx", None))

    return jax.shard_map(per_device, mesh=mesh, in_specs=in_specs, out_specs=out_specs, check_vma=False)
```

profile of v0, /device:TPU:0, one launch (start us, length us, event | category | flops | bytes accessed | tf_op | source)
XLA Modules:
  0.0 58.0 jit_solution(17942524390231201353)
XLA Ops:
  0.6 2.1 %shard_map.114 = (f32[16,8,128]{2,1,0:T(8,128)}, f32[32,8,128]{2,1,0:T(8,128)}, f32[25,8,128]{2,1,0:T(8,128)}, f32[25,8,128]{2,1,0:T(8,128)}, f32[25,8,128]{2,1,0:T(8,128)}, /*index=5*/f32[25,8,128]{2,1,0:T(8,128)}) custom-call(f32[8]{0:T(128)} %cond_t.1, f32[8]{0:T(128)} %store_t.1, f32[8,8,128]{2,1,0:T(8,128)} %previous.1, f32[8,8,128]{2,1,0:T(8,128)} %recharge.1, ...), custom_call_target="tpu_custom_call" | custom-call | flops 200000000 | bytes 4000000 | tf_op jit(solution)/shard_map/pallas_call | solution.py:447
  2.8 7.3 %all-to-all-start = ((f32[32,8,128]{2,1,0:T(8,128)}), f32[32,8,128]{2,1,0:T(8,128)S(1)}, u32[]{:S(2)}, u32[]{:S(2)}) async-start(f32[32,8,128]{2,1,0:T(8,128)} %get-tuple-element.25), calls=%async_computation | async-start | bytes 262144 | tf_op jit(solution)/shard_map/all_to_all | solution.py:500
  10.1 1.8 %collective-permute-start.2 = (f32[25,8,128]{2,1,0:T(8,128)}, f32[25,8,128]{2,1,0:T(8,128)S(1)}, u32[]{:S(2)}, u32[]{:S(2)}) collective-permute-start(f32[25,8,128]{2,1,0:T(8,128)} %get-tuple-element.34), channel_id=1, source_target_pairs={{0,1},{1,0},{2,3},{3,2},{4,5},{5,4},{6,7},{7,6},{8,9},{9,8},{10,11... | collective-permute-start | bytes 307208 | tf_op jit(solution)/shard_map/ppermute | solution.py:465
  11.9 2.4 %collective-permute-start.3 = (f32[25,8,128]{2,1,0:T(8,128)}, f32[25,8,128]{2,1,0:T(8,128)S(1)}, u32[]{:S(2)}, u32[]{:S(2)}) collective-permute-start(f32[25,8,128]{2,1,0:T(8,128)} %get-tuple-element.35), channel_id=1, source_target_pairs={{0,2},{1,3},{2,0},{3,1},{4,6},{5,7},{6,4},{7,5},{8,10},{9,11},{10,... | collective-permute-start | bytes 307208 | tf_op jit(solution)/shard_map/ppermute | solution.py:465
  14.6 1.5 %collective-permute-start.1 = (f32[16,8,128]{2,1,0:T(8,128)}, f32[16,8,128]{2,1,0:T(8,128)S(1)}, u32[]{:S(2)}, u32[]{:S(2)}) collective-permute-start(f32[16,8,128]{2,1,0:T(8,128)} %get-tuple-element.26), channel_id=1, source_target_pairs={{0,28},{4,0},{8,4},{12,8},{16,12},{20,16},{24,20},{28,24},{1,29},{... | collective-permute-start | bytes 196616 | tf_op jit(solution)/shard_map/ppermute | solution.py:460
  16.1 2.4 %collective-permute-done.1.below = f32[16,8,128]{2,1,0:T(8,128)S(1)} collective-permute-done((f32[16,8,128]{2,1,0:T(8,128)}, f32[16,8,128]{2,1,0:T(8,128)S(1)}, u32[]{:S(2)}, u32[]{:S(2)}) %collective-permute-start.1) | collective-permute-done | bytes 65568 | tf_op jit(solution)/shard_map/ppermute | solution.py:460
  18.6 2.4 %collective-permute-done.above = f32[16,8,128]{2,1,0:T(8,128)S(1)} collective-permute-done((f32[16,8,128]{2,1,0:T(8,128)}, f32[16,8,128]{2,1,0:T(8,128)S(1)}, u32[]{:S(2)}, u32[]{:S(2)}) %collective-permute-start) | collective-permute-done | bytes 65568 | tf_op jit(solution)/shard_map/ppermute | solution.py:460
  20.9 0.8 %copy-done.3 = f32[8,8,128]{2,1,0:T(8,128)S(1)} copy-done((f32[8,8,128]{2,1,0:T(8,128)S(1)}, f32[8,8,128]{2,1,0:T(8,128)}, u32[]{:S(2)}) %copy-start.3) | copy-done | bytes 32792
  21.7 0.8 %copy-done.4 = f32[8,8,128]{2,1,0:T(8,128)S(1)} copy-done((f32[8,8,128]{2,1,0:T(8,128)S(1)}, f32[8,8,128]{2,1,0:T(8,128)}, u32[]{:S(2)}) %copy-start.4) | copy-done | bytes 32792
  22.4 0.8 %copy-done.5 = s32[8,8,128]{2,1,0:T(8,128)S(1)} copy-done((s32[8,8,128]{2,1,0:T(8,128)S(1)}, s32[8,8,128]{2,1,0:T(8,128)}, u32[]{:S(2)}) %copy-start.5) | copy-done | bytes 32792
  23.2 0.7 %copy-done.8 = f32[8]{0:T(128)S(1)} copy-done((f32[8]{0:T(128)S(1)}, f32[8]{0:T(128)}, u32[]{:S(2)}) %copy-start.8) | copy-done | bytes 56
  23.8 0.7 %copy-done.9 = f32[8]{0:T(128)S(1)} copy-done((f32[8]{0:T(128)S(1)}, f32[8]{0:T(128)}, u32[]{:S(2)}) %copy-start.9) | copy-done | bytes 56
  24.5 3.2 %shard_map.115 = (f32[7,8,24,256]{3,2,1,0:T(8,128)S(1)}, f32[8,24,256]{2,1,0:T(8,128)S(1)}, f32[8,24,256]{2,1,0:T(8,128)S(1)}, f32[9,24,256]{2,1,0:T(8,128)S(1)}...) custom-call(f32[8]{0:T(128)S(1)} %copy-done.8, f32[8]{0:T(128)S(1)} %copy-done.9, f32[32,8,128]{2,1,0:T(8,128)S(1)} %all-to-all-done.sides, ...), custom_call_target="tpu_custom_call" | custom-call | flops 200000000 | bytes 4000000 | tf_op jit(solution)/shard_map/pallas_call | solution.py:447
  27.7 0.9 %copy-done = f32[25,8,128]{2,1,0:T(8,128)S(1)} copy-done((f32[25,8,128]{2,1,0:T(8,128)S(1)}, f32[25,8,128]{2,1,0:T(8,128)}, u32[]{:S(2)}) %copy-start) | copy-done | bytes 102424
  28.7 2.6 %collective-permute-start.6 = (f32[12,8,128]{2,1,0:T(8,128)S(1)}, f32[12,8,128]{2,1,0:T(8,128)S(1)}, u32[]{:S(2)}, u32[]{:S(2)}) collective-permute-start(f32[12,8,128]{2,1,0:T(8,128)S(1)} %get-tuple-element.38), channel_id=1, source_target_pairs={{0,28},{4,0},{8,4},{12,8},{16,12},{20,16},{24,20},{28,24},{1,29},{... | collective-permute-start | bytes 147464 | tf_op jit(solution)/shard_map/ppermute | solution.py:460
  31.4 3.7 %all-to-all-start.1 = ((f32[32,1,128]{2,1,0:T(1,128)}), f32[32,1,128]{2,1,0:T(1,128)S(1)}, u32[]{:S(2)}, u32[]{:S(2)}) async-start(f32[32,1,128]{2,1,0:T(1,128)} %bitcast.1), calls=%async_computation.1 | async-start | bytes 32768 | tf_op jit(solution)/shard_map/all_to_all | solution.py:516
  35.4 0.7 %shard_map.116.half_rates = f32[64,8,128]{2,1,0:T(8,128)S(1)} custom-call(f32[6,8]{1,0:T(8,128)S(1)} %copy-done.7, s32[8,8,128]{2,1,0:T(8,128)S(1)} %copy-done.6), custom_call_target="tpu_custom_call" | custom-call | flops 200000000 | bytes 4000000 | tf_op jit(solution)/shard_map/pallas_call | solution.py:447
  36.1 6.2 %all-to-all-done.1 = f32[32,1,128]{2,1,0:T(1,128)S(1)} async-done(((f32[32,1,128]{2,1,0:T(1,128)}), f32[32,1,128]{2,1,0:T(1,128)S(1)}, u32[]{:S(2)}, u32[]{:S(2)}) %all-to-all-start.1) | async-done | bytes 16416 | tf_op jit(solution)/shard_map/all_to_all | solution.py:516
  42.3 3.9 %shard_map.118 = (f32[8,8,128]{2,1,0:T(8,128)}, f32[24,8,128]{2,1,0:T(8,128)S(1)}, f32[24,8,128]{2,1,0:T(8,128)S(1)}, f32[24,8,128]{2,1,0:T(8,128)S(1)}, f32[24,8,128]{2,1,0:T(8,128)S(1)}) custom-call(f32[12,8]{1,0:T(8,128)S(1)} %copy.16.stoich, f32[8,8]{1,0:T(8,128)S(1)} %get-tuple-element.23.powers, f32[8,8]{1,0:T(8,128)S(1)} %get-tuple-element.24.products, ...), custom_call_target="tpu_custom_call" | custom-call | flops 200000000 | bytes 4000000 | tf_op jit(solution)/shard_map/pallas_call | solution.py:447
  46.7 0.6 %collective-permute-start.8 = (f32[24,8,128]{2,1,0:T(8,128)S(1)}, f32[24,8,128]{2,1,0:T(8,128)S(1)}, u32[]{:S(2)}, u32[]{:S(2)}) collective-permute-start(f32[24,8,128]{2,1,0:T(8,128)S(1)} %get-tuple-element.42), channel_id=1, source_target_pairs={{0,2},{1,3},{2,0},{3,1},{4,6},{5,7},{6,4},{7,5},{8,10},{9,11},{10,... | collective-permute-start | bytes 294920 | tf_op jit(solution)/shard_map/ppermute | solution.py:465
  47.3 3.3 %collective-permute-start.9 = (f32[24,8,128]{2,1,0:T(8,128)S(1)}, f32[24,8,128]{2,1,0:T(8,128)S(1)}, u32[]{:S(2)}, u32[]{:S(2)}) collective-permute-start(f32[24,8,128]{2,1,0:T(8,128)S(1)} %get-tuple-element.43), channel_id=1, source_target_pairs={{0,3},{1,2},{2,1},{3,0},{4,7},{5,6},{6,5},{7,4},{8,11},{9,10},{10,... | collective-permute-start | bytes 294920 | tf_op jit(solution)/shard_map/ppermute | solution.py:465
  50.6 1.3 %collective-permute-done.7.refs_1_ = f32[24,8,128]{2,1,0:T(8,128)S(1)} collective-permute-done((f32[24,8,128]{2,1,0:T(8,128)S(1)}, f32[24,8,128]{2,1,0:T(8,128)S(1)}, u32[]{:S(2)}, u32[]{:S(2)}) %collective-permute-start.7) | collective-permute-done | bytes 98336 | tf_op jit(solution)/shard_map/ppermute | solution.py:465
  51.9 5.3 %collective-permute-done.8.refs_2_ = f32[24,8,128]{2,1,0:T(8,128)S(1)} collective-permute-done((f32[24,8,128]{2,1,0:T(8,128)S(1)}, f32[24,8,128]{2,1,0:T(8,128)S(1)}, u32[]{:S(2)}, u32[]{:S(2)}) %collective-permute-start.8) | collective-permute-done | bytes 98336 | tf_op jit(solution)/shard_map/ppermute | solution.py:465
  57.2 0.8 %shard_map.119 = f32[3,8,8,512]{3,2,1,0:T(8,128)} custom-call(f32[24,8,128]{2,1,0:T(8,128)S(1)} %get-tuple-element.40.refs_0_, f32[24,8,128]{2,1,0:T(8,128)S(1)} %collective-permute-done.7.refs_1_, f32[24,8,128]{2,1,0:T(8,128)S(1)} %collective-permute-done.8.refs_2_, f32[24,8,128]{2,1,0:T(8,128)S(1)} %collective-permute-done.9.refs_3_), custom_call_target="tpu_custom_call" | custom-call | flops 200000000 | bytes 4000000 | tf_op jit(solution)/shard_map/pallas_call | solution.py:447
  (30 shorter events, 1.2 us)
Async XLA Ops:
  0.6 30.7 %copy-start.10 = (f32[12,8]{0,1:T(8,128)S(1)}, f32[12,8]{0,1:T(8,128)}, u32[]{:S(2)}) copy-start(f32[12,8]{0,1:T(8,128)} %param.18) | copy-start | bytes 1156
  2.7 32.7 %copy-start.6 = (s32[8,8,128]{2,1,0:T(8,128)S(1)}, s32[8,8,128]{2,1,0:T(8,128)}, u32[]{:S(2)}) copy-start(s32[8,8,128]{2,1,0:T(8,128)} %mineral.1) | copy-start | bytes 98308
  2.7 32.7 %copy-start.7 = (f32[6,8]{1,0:T(8,128)S(1)}, f32[6,8]{1,0:T(8,128)}, u32[]{:S(2)}) copy-start(f32[6,8]{1,0:T(8,128)} %rate_t.1) | copy-start | bytes 580
  2.8 18.2 %all-to-all-start = ((f32[32,8,128]{2,1,0:T(8,128)}), f32[32,8,128]{2,1,0:T(8,128)S(1)}, u32[]{:S(2)}, u32[]{:S(2)}) async-start(f32[32,8,128]{2,1,0:T(8,128)} %get-tuple-element.25), calls=%async_computation | async-start | bytes 262144 | tf_op jit(solution)/shard_map/all_to_all | solution.py:500
  10.1 17.6 %collective-permute-start.2 = (f32[25,8,128]{2,1,0:T(8,128)}, f32[25,8,128]{2,1,0:T(8,128)S(1)}, u32[]{:S(2)}, u32[]{:S(2)}) collective-permute-start(f32[25,8,128]{2,1,0:T(8,128)} %get-tuple-element.34), channel_id=1, source_target_pairs={{0,1},{1,0},{2,3},{3,2},{4,5},{5,4},{6,7},{7,6},{8,9},{9,8},{10,11... | collective-permute-start | bytes 307208 | tf_op jit(solution)/shard_map/ppermute | solution.py:465
  11.9 15.7 %collective-permute-start.3 = (f32[25,8,128]{2,1,0:T(8,128)}, f32[25,8,128]{2,1,0:T(8,128)S(1)}, u32[]{:S(2)}, u32[]{:S(2)}) collective-permute-start(f32[25,8,128]{2,1,0:T(8,128)} %get-tuple-element.35), channel_id=1, source_target_pairs={{0,2},{1,3},{2,0},{3,1},{4,6},{5,7},{6,4},{7,5},{8,10},{9,11},{10,... | collective-permute-start | bytes 307208 | tf_op jit(solution)/shard_map/ppermute | solution.py:465
  14.3 13.3 %collective-permute-start.4 = (f32[25,8,128]{2,1,0:T(8,128)}, f32[25,8,128]{2,1,0:T(8,128)S(1)}, u32[]{:S(2)}, u32[]{:S(2)}) collective-permute-start(f32[25,8,128]{2,1,0:T(8,128)} %get-tuple-element.36), channel_id=1, source_target_pairs={{0,3},{1,2},{2,1},{3,0},{4,7},{5,6},{6,5},{7,4},{8,11},{9,10},{10,... | collective-permute-start | bytes 307208 | tf_op jit(solution)/shard_map/ppermute | solution.py:465
  14.6 27.7 %copy-start.1 = (f32[25,8,128]{2,1,0:T(8,128)S(1)}, f32[25,8,128]{2,1,0:T(8,128)}, u32[]{:S(2)}) copy-start(f32[25,8,128]{2,1,0:T(8,128)} %get-tuple-element.33.refs_0_) | copy-start | bytes 307204
  14.6 27.7 %copy-start.2 = (f32[8]{0:T(128)S(1)}, f32[8]{0:T(128)}, u32[]{:S(2)}) copy-start(f32[8]{0:T(128)} %log_equil.1) | copy-start | bytes 100
  14.6 4.0 %collective-permute-start.1 = (f32[16,8,128]{2,1,0:T(8,128)}, f32[16,8,128]{2,1,0:T(8,128)S(1)}, u32[]{:S(2)}, u32[]{:S(2)}) collective-permute-start(f32[16,8,128]{2,1,0:T(8,128)} %get-tuple-element.26), channel_id=1, source_target_pairs={{0,28},{4,0},{8,4},{12,8},{16,12},{20,16},{24,20},{28,24},{1,29},{... | collective-permute-start | bytes 196616 | tf_op jit(solution)/shard_map/ppermute | solution.py:460
  16.1 4.8 %collective-permute-start = (f32[16,8,128]{2,1,0:T(8,128)}, f32[16,8,128]{2,1,0:T(8,128)S(1)}, u32[]{:S(2)}, u32[]{:S(2)}) collective-permute-start(f32[16,8,128]{2,1,0:T(8,128)} %get-tuple-element.26), channel_id=1, source_target_pairs={{0,4},{4,8},{8,12},{12,16},{16,20},{20,24},{24,28},{28,0},{1,5},{5... | collective-permute-start | bytes 196616 | tf_op jit(solution)/shard_map/ppermute | solution.py:460
  20.9 0.8 %copy-start.3 = (f32[8,8,128]{2,1,0:T(8,128)S(1)}, f32[8,8,128]{2,1,0:T(8,128)}, u32[]{:S(2)}) copy-start(f32[8,8,128]{2,1,0:T(8,128)} %previous.1) | copy-start | bytes 98308
  21.7 0.8 %copy-start.4 = (f32[8,8,128]{2,1,0:T(8,128)S(1)}, f32[8,8,128]{2,1,0:T(8,128)}, u32[]{:S(2)}) copy-start(f32[8,8,128]{2,1,0:T(8,128)} %recharge.1) | copy-start | bytes 98308
  22.4 0.8 %copy-start.5 = (s32[8,8,128]{2,1,0:T(8,128)S(1)}, s32[8,8,128]{2,1,0:T(8,128)}, u32[]{:S(2)}) copy-start(s32[8,8,128]{2,1,0:T(8,128)} %zone.1) | copy-start | bytes 98308
  23.2 0.7 %copy-start.8 = (f32[8]{0:T(128)S(1)}, f32[8]{0:T(128)}, u32[]{:S(2)}) copy-start(f32[8]{0:T(128)} %cond_t.1) | copy-start | bytes 100
  23.8 0.7 %copy-start.9 = (f32[8]{0:T(128)S(1)}, f32[8]{0:T(128)}, u32[]{:S(2)}) copy-start(f32[8]{0:T(128)} %store_t.1) | copy-start | bytes 100
  27.7 0.9 %copy-start = (f32[25,8,128]{2,1,0:T(8,128)S(1)}, f32[25,8,128]{2,1,0:T(8,128)}, u32[]{:S(2)}) copy-start(f32[25,8,128]{2,1,0:T(8,128)} %get-tuple-element.33.refs_0_) | copy-start | bytes 307204
  28.6 13.7 %collective-permute-start.5 = (f32[12,8,128]{2,1,0:T(8,128)S(1)}, f32[12,8,128]{2,1,0:T(8,128)S(1)}, u32[]{:S(2)}, u32[]{:S(2)}) collective-permute-start(f32[12,8,128]{2,1,0:T(8,128)S(1)} %get-tuple-element.37), channel_id=1, source_target_pairs={{0,4},{4,8},{8,12},{12,16},{16,20},{20,24},{24,28},{28,0},{1,5},{5... | collective-permute-start | bytes 147464 | tf_op jit(solution)/shard_map/ppermute | solution.py:460
  28.7 13.6 %collective-permute-start.6 = (f32[12,8,128]{2,1,0:T(8,128)S(1)}, f32[12,8,128]{2,1,0:T(8,128)S(1)}, u32[]{:S(2)}, u32[]{:S(2)}) collective-permute-start(f32[12,8,128]{2,1,0:T(8,128)S(1)} %get-tuple-element.38), channel_id=1, source_target_pairs={{0,28},{4,0},{8,4},{12,8},{16,12},{20,16},{24,20},{28,24},{1,29},{... | collective-permute-start | bytes 147464 | tf_op jit(solution)/shard_map/ppermute | solution.py:460
  31.4 10.9 %all-to-all-start.1 = ((f32[32,1,128]{2,1,0:T(1,128)}), f32[32,1,128]{2,1,0:T(1,128)S(1)}, u32[]{:S(2)}, u32[]{:S(2)}) async-start(f32[32,1,128]{2,1,0:T(1,128)} %bitcast.1), calls=%async_computation.1 | async-start | bytes 32768 | tf_op jit(solution)/shard_map/all_to_all | solution.py:516
  46.2 5.7 %collective-permute-start.7 = (f32[24,8,128]{2,1,0:T(8,128)S(1)}, f32[24,8,128]{2,1,0:T(8,128)S(1)}, u32[]{:S(2)}, u32[]{:S(2)}) collective-permute-start(f32[24,8,128]{2,1,0:T(8,128)S(1)} %get-tuple-element.41), channel_id=1, source_target_pairs={{0,1},{1,0},{2,3},{3,2},{4,5},{5,4},{6,7},{7,6},{8,9},{9,8},{10,11... | collective-permute-start | bytes 294920 | tf_op jit(solution)/shard_map/ppermute | solution.py:465
  46.7 10.5 %collective-permute-start.8 = (f32[24,8,128]{2,1,0:T(8,128)S(1)}, f32[24,8,128]{2,1,0:T(8,128)S(1)}, u32[]{:S(2)}, u32[]{:S(2)}) collective-permute-start(f32[24,8,128]{2,1,0:T(8,128)S(1)} %get-tuple-element.42), channel_id=1, source_target_pairs={{0,2},{1,3},{2,0},{3,1},{4,6},{5,7},{6,4},{7,5},{8,10},{9,11},{10,... | collective-permute-start | bytes 294920 | tf_op jit(solution)/shard_map/ppermute | solution.py:465
  47.3 9.8 %collective-permute-start.9 = (f32[24,8,128]{2,1,0:T(8,128)S(1)}, f32[24,8,128]{2,1,0:T(8,128)S(1)}, u32[]{:S(2)}, u32[]{:S(2)}) collective-permute-start(f32[24,8,128]{2,1,0:T(8,128)S(1)} %get-tuple-element.43), channel_id=1, source_target_pairs={{0,3},{1,2},{2,1},{3,0},{4,7},{5,6},{6,5},{7,4},{8,11},{9,10},{10,... | collective-permute-start | bytes 294920 | tf_op jit(solution)/shard_map/ppermute | solution.py:465
where the time goes:
time: 58.5 us; the launch traced here: 58 us
  starting transfers between devices  24.1 us (41%)
  waiting for transfers between devices  17.5 us (30%)
  Pallas kernels  11 us (19%)
  local copies, waits for them, and re-layouts  4.58 us (8%)
  between operations  0.74 us (1%)
    pallas_call x7, Pallas kernels, call(): pl.pallas_call(kernel, out_shape=shapes, in_specs=[smem] * len(tables) +...  11 us
    ppermute x6, starting transfers between devices, swapped(): return lax.ppermute(array, axis, [(i, i ^ mask) for i in range(count)])  8.84 us
    all_to_all x1, starting transfers between devices, per_device(): sides = lax.all_to_all(sides, everywhere, 0, 0, tiled=True)  7.33 us
    ppermute x6, waiting for transfers between devices, swapped(): return lax.ppermute(array, axis, [(i, i ^ mask) for i in range(count)])  6.58 us
    all_to_all x1, waiting for transfers between devices, per_device(): sums = lax.all_to_all(sums, everywhere, 0, 0, tiled=True)  6.16 us
    ppermute x4, waiting for transfers between devices, shifted(): lax.ppermute(array, axis, [(i, (i + amount) % count) for i in range(count)])  4.8 us
    unnamed x23, local copies, waits for them, and re-layouts  4.58 us
    ppermute x4, starting transfers between devices, shifted(): lax.ppermute(array, axis, [(i, (i + amount) % count) for i in range(count)])  4.24 us
  transfers between devices with their start and end apart: 12, of which 5 were waited for; matrix products, arithmetic and copies ran while one was open for 0% of the time, Pallas kernels for 7%

commit v1 on v0

--- a/solution.py
+++ b/solution.py
@@ -21,7 +21,7 @@
 WHOLE_VMEM_BYTES = 60 * 1024 * 1024
 BASIS = ITERS + 1
 HALO = ITERS + 1
-LAYERS_TOGETHER = 4
+LAYERS_TOGETHER = 8
 PAIRS = [(i, j) for j in range(BASIS) for i in range(j + 1)]
 PAIR_AT = {pair: at for at, pair in enumerate(PAIRS)}
 PAIR_ROWS = -(-len(PAIRS) // 8) * 8
@@ -116,10 +116,8 @@
             for z in range(layers):
                 j = c * layers + z
                 blocks[d][j] = species[c, z, :, at[1]]
-                edge = jnp.where(lane == 2 * j, pltpu.roll(species[c, z, :, at[2]], 2 * j, 1), edge)
-                edge = jnp.where(
-                    lane == 2 * j + 1, pltpu.roll(species[c, z, :, at[0]], 2 * j + 2, 1), edge
-                )
+                ends = jnp.where(lane == 0, species[c, z, :, at[2]], species[c, z, :, at[0]])
+                edge = jnp.where(jnp.right_shift(lane, 1) == j, pltpu.roll(ends, 2 * j + 1, 1), edge)
         blocks[d][groups * layers] = edge
 
 
@@ -296,20 +294,21 @@
     for newton_pass in range(NEWTON):
         affinity = first
         if shift is not None:
-            affinity = [value - newton_damping * past for value, past in zip(first, image)]
+            affinity = [value - past for value, past in zip(first, image)]
         tangent = [jnp.tanh(value) for value in affinity]
         gap = [rate * value for rate, value in zip(half_rates, tangent)]
         if shift is not None:
             gap = [value - past for value, past in zip(gap, shift)]
+        gap = [newton_damping * value for value in gap]
         weight = [rate * (1.0 - value * value) for rate, value in zip(half_rates, tangent)]
         matrix = {(i, j): powers[i, j] for i in range(minerals) for j in range(i + 1)}
-        inverse, ahead, drawn = [], [], [None] * minerals
+        ahead, factors, drawn = [], [], [None] * minerals
         for k in range(minerals):
             scaled = 1.0 / (1.0 + weight[k] * matrix[(k, k)])
-            inverse.append(scaled)
             left = gap[k] if k == 0 else gap[k] - weight[k] * drawn[k]
             ahead.append(left * scaled)
             factor = weight[k] * scaled
+            factors.append(factor)
             for i in range(k + 1, minerals):
                 term = matrix[(i, k)] * ahead[k]
                 drawn[i] = term if k == 0 else drawn[i] + term
@@ -327,12 +326,11 @@
             for j in range(k + 1, minerals):
                 term = matrix[(j, k)] * step[j]
                 total = term if total is None else total + term
-            step[k] = ahead[k] if total is None else ahead[k] - weight[k] * inverse[k] * total
+            step[k] = ahead[k] if total is None else ahead[k] - factors[k] * total
             if newton_pass + 1 < NEWTON:
                 parts = [part for part in (drawn[k], total) if part is not None]
                 image[k] = sum(parts, matrix[(k, k)] * step[k])
-        delta = [newton_damping * value for value in step]
-        shift = delta if shift is None else [past + value for past, value in zip(shift, delta)]
+        shift = step if shift is None else [past + value for past, value in zip(shift, step)]
     result = []
     for value, row in zip(moved, rows):
         for m in range(minerals):
@@ -408,14 +406,16 @@
             for c in range(groups):
                 at = c * layers
                 here = block[pl.ds(at + z, together)]
-                side = jnp.stack([pltpu.roll(edge, LANES - 1 - 2 * (at + z + u), 1) for u in range(together)])
+                last = [pltpu.roll(edge, LANES - 2 - 2 * (at + z + u), 1) for u in range(together)]
+                first = jnp.stack([pltpu.roll(value, 2, 1) for value in last])
+                last = jnp.stack(last)
                 edge_at = d * groups + c
                 lines = [ref[edge_at, here_at, :][:, None, :] for ref in (below, above)]
                 following = jnp.where(row == rows - 1, lines[0], pltpu.roll(here, rows - 1, 1))
                 preceding = jnp.where(row == 0, lines[1], pltpu.roll(here, 1, 1))
                 result = stay * here + inward[0] * following + inward[1] * preceding
-                result = result + inward[2] * jnp.where(lane == LANES - 1, side, pltpu.roll(here, LANES - 1, 2))
-                result = result + inward[3] * jnp.where(lane == 0, side, pltpu.roll(here, 1, 2))
+                result = result + inward[2] * jnp.where(lane == LANES - 1, last, pltpu.roll(here, LANES - 1, 2))
+                result = result + inward[3] * jnp.where(lane == 0, first, pltpu.roll(here, 1, 2))
                 over, under = beside(block, at, here)
                 moved.append(result + inward[4] * over + inward[5] * under)
                 table_rows.append(group * groups + c)
@@ -526,7 +526,9 @@
         [(layers,) + tile] + [(groups * layers,) + tile] * count,
         [extended, (PAIR_ROWS, LANES)],
     )
-    arrived = {d: swapped(reacted[d], "sp", d) for d in range(count - 1, 0, -1)}
+    arrived = {}
+    for d in range(1, count):
+        arrived[d] = swapped(reacted[d], "sp", d)
     (species_out,) = call(place_kernel, [], [reacted[0]] + [arrived[d] for d in range(1, count)], [species.shape])
     return (head_field, species_out)
 

time: 58.5 us -> 58.3 us (level)
  no operation moved by 1% of the time
where the time goes in v1:
time: 58.3 us; the launch traced here: 57.7 us
  starting transfers between devices  24.1 us (41%)
  waiting for transfers between devices  17.5 us (30%)
  Pallas kernels  10.7 us (18%)
  local copies, waits for them, and re-layouts  4.58 us (8%)
  between operations  0.74 us (1%)
    pallas_call x7, Pallas kernels, call(): pl.pallas_call(kernel, out_shape=shapes, in_specs=[smem] * len(tables) +...  10.7 us
    ppermute x6, starting transfers between devices, swapped(): return lax.ppermute(array, axis, [(i, i ^ mask) for i in range(count)])  8.84 us
    all_to_all x1, starting transfers between devices, per_device(): sides = lax.all_to_all(sides, everywhere, 0, 0, tiled=True)  7.33 us
    ppermute x6, waiting for transfers between devices, swapped(): return lax.ppermute(array, axis, [(i, i ^ mask) for i in range(count)])  6.58 us
    all_to_all x1, waiting for transfers between devices, per_device(): sums = lax.all_to_all(sums, everywhere, 0, 0, tiled=True)  6.16 us
    ppermute x4, waiting for transfers between devices, shifted(): lax.ppermute(array, axis, [(i, (i + amount) % count) for i in range(count)])  4.8 us
    unnamed x23, local copies, waits for them, and re-layouts  4.58 us
    ppermute x4, starting transfers between devices, shifted(): lax.ppermute(array, axis, [(i, (i + amount) % count) for i in range(count)])  4.24 us
  transfers between devices with their start and end apart: 12, of which 5 were waited for; matrix products, arithmetic and copies ran while one was open for 0% of the time, Pallas kernels for 7%

profile of v1, /device:TPU:0, one launch (start us, length us, event | category | flops | bytes accessed | tf_op | source)
XLA Modules:
  0.0 57.7 jit_solution(8666835143754957616)
XLA Ops:
  0.6 2.0 %shard_map.114 = (f32[16,8,128]{2,1,0:T(8,128)}, f32[32,8,128]{2,1,0:T(8,128)}, f32[25,8,128]{2,1,0:T(8,128)}, f32[25,8,128]{2,1,0:T(8,128)}, f32[25,8,128]{2,1,0:T(8,128)}, /*index=5*/f32[25,8,128]{2,1,0:T(8,128)}) custom-call(f32[8]{0:T(128)} %cond_t.1, f32[8]{0:T(128)} %store_t.1, f32[8,8,128]{2,1,0:T(8,128)} %previous.1, f32[8,8,128]{2,1,0:T(8,128)} %recharge.1, ...), custom_call_target="tpu_custom_call" | custom-call | flops 200000000 | bytes 4000000 | tf_op jit(solution)/shard_map/pallas_call | solution.py:447
  2.7 7.3 %all-to-all-start = ((f32[32,8,128]{2,1,0:T(8,128)}), f32[32,8,128]{2,1,0:T(8,128)S(1)}, u32[]{:S(2)}, u32[]{:S(2)}) async-start(f32[32,8,128]{2,1,0:T(8,128)} %get-tuple-element.25), calls=%async_computation | async-start | bytes 262144 | tf_op jit(solution)/shard_map/all_to_all | solution.py:500
  10.1 1.8 %collective-permute-start.2 = (f32[25,8,128]{2,1,0:T(8,128)}, f32[25,8,128]{2,1,0:T(8,128)S(1)}, u32[]{:S(2)}, u32[]{:S(2)}) collective-permute-start(f32[25,8,128]{2,1,0:T(8,128)} %get-tuple-element.34), channel_id=1, source_target_pairs={{0,1},{1,0},{2,3},{3,2},{4,5},{5,4},{6,7},{7,6},{8,9},{9,8},{10,11... | collective-permute-start | bytes 307208 | tf_op jit(solution)/shard_map/ppermute | solution.py:465
  11.9 2.4 %collective-permute-start.3 = (f32[25,8,128]{2,1,0:T(8,128)}, f32[25,8,128]{2,1,0:T(8,128)S(1)}, u32[]{:S(2)}, u32[]{:S(2)}) collective-permute-start(f32[25,8,128]{2,1,0:T(8,128)} %get-tuple-element.35), channel_id=1, source_target_pairs={{0,2},{1,3},{2,0},{3,1},{4,6},{5,7},{6,4},{7,5},{8,10},{9,11},{10,... | collective-permute-start | bytes 307208 | tf_op jit(solution)/shard_map/ppermute | solution.py:465
  14.5 1.5 %collective-permute-start.1 = (f32[16,8,128]{2,1,0:T(8,128)}, f32[16,8,128]{2,1,0:T(8,128)S(1)}, u32[]{:S(2)}, u32[]{:S(2)}) collective-permute-start(f32[16,8,128]{2,1,0:T(8,128)} %get-tuple-element.26), channel_id=1, source_target_pairs={{0,28},{4,0},{8,4},{12,8},{16,12},{20,16},{24,20},{28,24},{1,29},{... | collective-permute-start | bytes 196616 | tf_op jit(solution)/shard_map/ppermute | solution.py:460
  16.1 2.4 %collective-permute-done.1.below = f32[16,8,128]{2,1,0:T(8,128)S(1)} collective-permute-done((f32[16,8,128]{2,1,0:T(8,128)}, f32[16,8,128]{2,1,0:T(8,128)S(1)}, u32[]{:S(2)}, u32[]{:S(2)}) %collective-permute-start.1) | collective-permute-done | bytes 65568 | tf_op jit(solution)/shard_map/ppermute | solution.py:460
  18.5 2.4 %collective-permute-done.above = f32[16,8,128]{2,1,0:T(8,128)S(1)} collective-permute-done((f32[16,8,128]{2,1,0:T(8,128)}, f32[16,8,128]{2,1,0:T(8,128)S(1)}, u32[]{:S(2)}, u32[]{:S(2)}) %collective-permute-start) | collective-permute-done | bytes 65568 | tf_op jit(solution)/shard_map/ppermute | solution.py:460
  20.9 0.8 %copy-done.3 = f32[8,8,128]{2,1,0:T(8,128)S(1)} copy-done((f32[8,8,128]{2,1,0:T(8,128)S(1)}, f32[8,8,128]{2,1,0:T(8,128)}, u32[]{:S(2)}) %copy-start.3) | copy-done | bytes 32792
  21.6 0.8 %copy-done.4 = f32[8,8,128]{2,1,0:T(8,128)S(1)} copy-done((f32[8,8,128]{2,1,0:T(8,128)S(1)}, f32[8,8,128]{2,1,0:T(8,128)}, u32[]{:S(2)}) %copy-start.4) | copy-done | bytes 32792
  22.4 0.8 %copy-done.5 = s32[8,8,128]{2,1,0:T(8,128)S(1)} copy-done((s32[8,8,128]{2,1,0:T(8,128)S(1)}, s32[8,8,128]{2,1,0:T(8,128)}, u32[]{:S(2)}) %copy-start.5) | copy-done | bytes 32792
  23.1 0.7 %copy-done.8 = f32[8]{0:T(128)S(1)} copy-done((f32[8]{0:T(128)S(1)}, f32[8]{0:T(128)}, u32[]{:S(2)}) %copy-start.8) | copy-done | bytes 56
  23.8 0.7 %copy-done.9 = f32[8]{0:T(128)S(1)} copy-done((f32[8]{0:T(128)S(1)}, f32[8]{0:T(128)}, u32[]{:S(2)}) %copy-start.9) | copy-done | bytes 56
  24.5 3.2 %shard_map.115 = (f32[7,8,24,256]{3,2,1,0:T(8,128)S(1)}, f32[8,24,256]{2,1,0:T(8,128)S(1)}, f32[8,24,256]{2,1,0:T(8,128)S(1)}, f32[9,24,256]{2,1,0:T(8,128)S(1)}...) custom-call(f32[8]{0:T(128)S(1)} %copy-done.8, f32[8]{0:T(128)S(1)} %copy-done.9, f32[32,8,128]{2,1,0:T(8,128)S(1)} %all-to-all-done.sides, ...), custom_call_target="tpu_custom_call" | custom-call | flops 200000000 | bytes 4000000 | tf_op jit(solution)/shard_map/pallas_call | solution.py:447
  27.6 0.9 %copy-done = f32[25,8,128]{2,1,0:T(8,128)S(1)} copy-done((f32[25,8,128]{2,1,0:T(8,128)S(1)}, f32[25,8,128]{2,1,0:T(8,128)}, u32[]{:S(2)}) %copy-start) | copy-done | bytes 102424
  28.6 2.6 %collective-permute-start.6 = (f32[12,8,128]{2,1,0:T(8,128)S(1)}, f32[12,8,128]{2,1,0:T(8,128)S(1)}, u32[]{:S(2)}, u32[]{:S(2)}) collective-permute-start(f32[12,8,128]{2,1,0:T(8,128)S(1)} %get-tuple-element.38), channel_id=1, source_target_pairs={{0,28},{4,0},{8,4},{12,8},{16,12},{20,16},{24,20},{28,24},{1,29},{... | collective-permute-start | bytes 147464 | tf_op jit(solution)/shard_map/ppermute | solution.py:460
  31.4 3.7 %all-to-all-start.1 = ((f32[32,1,128]{2,1,0:T(1,128)}), f32[32,1,128]{2,1,0:T(1,128)S(1)}, u32[]{:S(2)}, u32[]{:S(2)}) async-start(f32[32,1,128]{2,1,0:T(1,128)} %bitcast.1), calls=%async_computation.1 | async-start | bytes 32768 | tf_op jit(solution)/shard_map/all_to_all | solution.py:516
  35.4 0.7 %shard_map.116.half_rates = f32[64,8,128]{2,1,0:T(8,128)S(1)} custom-call(f32[6,8]{1,0:T(8,128)S(1)} %copy-done.7, s32[8,8,128]{2,1,0:T(8,128)S(1)} %copy-done.6), custom_call_target="tpu_custom_call" | custom-call | flops 200000000 | bytes 4000000 | tf_op jit(solution)/shard_map/pallas_call | solution.py:447
  36.1 6.2 %all-to-all-done.1 = f32[32,1,128]{2,1,0:T(1,128)S(1)} async-done(((f32[32,1,128]{2,1,0:T(1,128)}), f32[32,1,128]{2,1,0:T(1,128)S(1)}, u32[]{:S(2)}, u32[]{:S(2)}) %all-to-all-start.1) | async-done | bytes 16416 | tf_op jit(solution)/shard_map/all_to_all | solution.py:516
  42.3 3.7 %shard_map.118 = (f32[8,8,128]{2,1,0:T(8,128)}, f32[24,8,128]{2,1,0:T(8,128)S(1)}, f32[24,8,128]{2,1,0:T(8,128)S(1)}, f32[24,8,128]{2,1,0:T(8,128)S(1)}, f32[24,8,128]{2,1,0:T(8,128)S(1)}) custom-call(f32[12,8]{1,0:T(8,128)S(1)} %copy.16.stoich, f32[8,8]{1,0:T(8,128)S(1)} %get-tuple-element.23.powers, f32[8,8]{1,0:T(8,128)S(1)} %get-tuple-element.24.products, ...), custom_call_target="tpu_custom_call" | custom-call | flops 200000000 | bytes 4000000 | tf_op jit(solution)/shard_map/pallas_call | solution.py:447
  46.5 0.6 %collective-permute-start.8 = (f32[24,8,128]{2,1,0:T(8,128)S(1)}, f32[24,8,128]{2,1,0:T(8,128)S(1)}, u32[]{:S(2)}, u32[]{:S(2)}) collective-permute-start(f32[24,8,128]{2,1,0:T(8,128)S(1)} %get-tuple-element.42), channel_id=1, source_target_pairs={{0,2},{1,3},{2,0},{3,1},{4,6},{5,7},{6,4},{7,5},{8,10},{9,11},{10,... | collective-permute-start | bytes 294920 | tf_op jit(solution)/shard_map/ppermute | solution.py:465
  47.1 3.3 %collective-permute-start.9 = (f32[24,8,128]{2,1,0:T(8,128)S(1)}, f32[24,8,128]{2,1,0:T(8,128)S(1)}, u32[]{:S(2)}, u32[]{:S(2)}) collective-permute-start(f32[24,8,128]{2,1,0:T(8,128)S(1)} %get-tuple-element.43), channel_id=1, source_target_pairs={{0,3},{1,2},{2,1},{3,0},{4,7},{5,6},{6,5},{7,4},{8,11},{9,10},{10,... | collective-permute-start | bytes 294920 | tf_op jit(solution)/shard_map/ppermute | solution.py:465
  50.4 1.3 %collective-permute-done.7.refs_1_ = f32[24,8,128]{2,1,0:T(8,128)S(1)} collective-permute-done((f32[24,8,128]{2,1,0:T(8,128)S(1)}, f32[24,8,128]{2,1,0:T(8,128)S(1)}, u32[]{:S(2)}, u32[]{:S(2)}) %collective-permute-start.7) | collective-permute-done | bytes 98336 | tf_op jit(solution)/shard_map/ppermute | solution.py:465
  51.7 5.3 %collective-permute-done.8.refs_2_ = f32[24,8,128]{2,1,0:T(8,128)S(1)} collective-permute-done((f32[24,8,128]{2,1,0:T(8,128)S(1)}, f32[24,8,128]{2,1,0:T(8,128)S(1)}, u32[]{:S(2)}, u32[]{:S(2)}) %collective-permute-start.8) | collective-permute-done | bytes 98336 | tf_op jit(solution)/shard_map/ppermute | solution.py:465
  56.9 0.8 %shard_map.119 = f32[3,8,8,512]{3,2,1,0:T(8,128)} custom-call(f32[24,8,128]{2,1,0:T(8,128)S(1)} %get-tuple-element.40.refs_0_, f32[24,8,128]{2,1,0:T(8,128)S(1)} %collective-permute-done.7.refs_1_, f32[24,8,128]{2,1,0:T(8,128)S(1)} %collective-permute-done.8.refs_2_, f32[24,8,128]{2,1,0:T(8,128)S(1)} %collective-permute-done.9.refs_3_), custom_call_target="tpu_custom_call" | custom-call | flops 200000000 | bytes 4000000 | tf_op jit(solution)/shard_map/pallas_call | solution.py:447
  (30 shorter events, 1.2 us)
Async XLA Ops:
  0.6 30.7 %copy-start.10 = (f32[12,8]{0,1:T(8,128)S(1)}, f32[12,8]{0,1:T(8,128)}, u32[]{:S(2)}) copy-start(f32[12,8]{0,1:T(8,128)} %param.18) | copy-start | bytes 1156
  2.7 32.7 %copy-start.6 = (s32[8,8,128]{2,1,0:T(8,128)S(1)}, s32[8,8,128]{2,1,0:T(8,128)}, u32[]{:S(2)}) copy-start(s32[8,8,128]{2,1,0:T(8,128)} %mineral.1) | copy-start | bytes 98308
  2.7 32.7 %copy-start.7 = (f32[6,8]{1,0:T(8,128)S(1)}, f32[6,8]{1,0:T(8,128)}, u32[]{:S(2)}) copy-start(f32[6,8]{1,0:T(8,128)} %rate_t.1) | copy-start | bytes 580
  2.7 18.2 %all-to-all-start = ((f32[32,8,128]{2,1,0:T(8,128)}), f32[32,8,128]{2,1,0:T(8,128)S(1)}, u32[]{:S(2)}, u32[]{:S(2)}) async-start(f32[32,8,128]{2,1,0:T(8,128)} %get-tuple-element.25), calls=%async_computation | async-start | bytes 262144 | tf_op jit(solution)/shard_map/all_to_all | solution.py:500
  10.1 17.6 %collective-permute-start.2 = (f32[25,8,128]{2,1,0:T(8,128)}, f32[25,8,128]{2,1,0:T(8,128)S(1)}, u32[]{:S(2)}, u32[]{:S(2)}) collective-permute-start(f32[25,8,128]{2,1,0:T(8,128)} %get-tuple-element.34), channel_id=1, source_target_pairs={{0,1},{1,0},{2,3},{3,2},{4,5},{5,4},{6,7},{7,6},{8,9},{9,8},{10,11... | collective-permute-start | bytes 307208 | tf_op jit(solution)/shard_map/ppermute | solution.py:465
  11.9 15.7 %collective-permute-start.3 = (f32[25,8,128]{2,1,0:T(8,128)}, f32[25,8,128]{2,1,0:T(8,128)S(1)}, u32[]{:S(2)}, u32[]{:S(2)}) collective-permute-start(f32[25,8,128]{2,1,0:T(8,128)} %get-tuple-element.35), channel_id=1, source_target_pairs={{0,2},{1,3},{2,0},{3,1},{4,6},{5,7},{6,4},{7,5},{8,10},{9,11},{10,... | collective-permute-start | bytes 307208 | tf_op jit(solution)/shard_map/ppermute | solution.py:465
  14.3 13.3 %collective-permute-start.4 = (f32[25,8,128]{2,1,0:T(8,128)}, f32[25,8,128]{2,1,0:T(8,128)S(1)}, u32[]{:S(2)}, u32[]{:S(2)}) collective-permute-start(f32[25,8,128]{2,1,0:T(8,128)} %get-tuple-element.36), channel_id=1, source_target_pairs={{0,3},{1,2},{2,1},{3,0},{4,7},{5,6},{6,5},{7,4},{8,11},{9,10},{10,... | collective-permute-start | bytes 307208 | tf_op jit(solution)/shard_map/ppermute | solution.py:465
  14.5 27.7 %copy-start.1 = (f32[25,8,128]{2,1,0:T(8,128)S(1)}, f32[25,8,128]{2,1,0:T(8,128)}, u32[]{:S(2)}) copy-start(f32[25,8,128]{2,1,0:T(8,128)} %get-tuple-element.33.refs_0_) | copy-start | bytes 307204
  14.5 27.7 %copy-start.2 = (f32[8]{0:T(128)S(1)}, f32[8]{0:T(128)}, u32[]{:S(2)}) copy-start(f32[8]{0:T(128)} %log_equil.1) | copy-start | bytes 100
  14.5 4.0 %collective-permute-start.1 = (f32[16,8,128]{2,1,0:T(8,128)}, f32[16,8,128]{2,1,0:T(8,128)S(1)}, u32[]{:S(2)}, u32[]{:S(2)}) collective-permute-start(f32[16,8,128]{2,1,0:T(8,128)} %get-tuple-element.26), channel_id=1, source_target_pairs={{0,28},{4,0},{8,4},{12,8},{16,12},{20,16},{24,20},{28,24},{1,29},{... | collective-permute-start | bytes 196616 | tf_op jit(solution)/shard_map/ppermute | solution.py:460
  16.1 4.8 %collective-permute-start = (f32[16,8,128]{2,1,0:T(8,128)}, f32[16,8,128]{2,1,0:T(8,128)S(1)}, u32[]{:S(2)}, u32[]{:S(2)}) collective-permute-start(f32[16,8,128]{2,1,0:T(8,128)} %get-tuple-element.26), channel_id=1, source_target_pairs={{0,4},{4,8},{8,12},{12,16},{16,20},{20,24},{24,28},{28,0},{1,5},{5... | collective-permute-start | bytes 196616 | tf_op jit(solution)/shard_map/ppermute | solution.py:460
  20.9 0.8 %copy-start.3 = (f32[8,8,128]{2,1,0:T(8,128)S(1)}, f32[8,8,128]{2,1,0:T(8,128)}, u32[]{:S(2)}) copy-start(f32[8,8,128]{2,1,0:T(8,128)} %previous.1) | copy-start | bytes 98308
  21.6 0.8 %copy-start.4 = (f32[8,8,128]{2,1,0:T(8,128)S(1)}, f32[8,8,128]{2,1,0:T(8,128)}, u32[]{:S(2)}) copy-start(f32[8,8,128]{2,1,0:T(8,128)} %recharge.1) | copy-start | bytes 98308
  22.4 0.8 %copy-start.5 = (s32[8,8,128]{2,1,0:T(8,128)S(1)}, s32[8,8,128]{2,1,0:T(8,128)}, u32[]{:S(2)}) copy-start(s32[8,8,128]{2,1,0:T(8,128)} %zone.1) | copy-start | bytes 98308
  23.1 0.7 %copy-start.8 = (f32[8]{0:T(128)S(1)}, f32[8]{0:T(128)}, u32[]{:S(2)}) copy-start(f32[8]{0:T(128)} %cond_t.1) | copy-start | bytes 100
  23.8 0.7 %copy-start.9 = (f32[8]{0:T(128)S(1)}, f32[8]{0:T(128)}, u32[]{:S(2)}) copy-start(f32[8]{0:T(128)} %store_t.1) | copy-start | bytes 100
  27.6 0.9 %copy-start = (f32[25,8,128]{2,1,0:T(8,128)S(1)}, f32[25,8,128]{2,1,0:T(8,128)}, u32[]{:S(2)}) copy-start(f32[25,8,128]{2,1,0:T(8,128)} %get-tuple-element.33.refs_0_) | copy-start | bytes 307204
  28.6 13.7 %collective-permute-start.5 = (f32[12,8,128]{2,1,0:T(8,128)S(1)}, f32[12,8,128]{2,1,0:T(8,128)S(1)}, u32[]{:S(2)}, u32[]{:S(2)}) collective-permute-start(f32[12,8,128]{2,1,0:T(8,128)S(1)} %get-tuple-element.37), channel_id=1, source_target_pairs={{0,4},{4,8},{8,12},{12,16},{16,20},{20,24},{24,28},{28,0},{1,5},{5... | collective-permute-start | bytes 147464 | tf_op jit(solution)/shard_map/ppermute | solution.py:460
  28.6 13.6 %collective-permute-start.6 = (f32[12,8,128]{2,1,0:T(8,128)S(1)}, f32[12,8,128]{2,1,0:T(8,128)S(1)}, u32[]{:S(2)}, u32[]{:S(2)}) collective-permute-start(f32[12,8,128]{2,1,0:T(8,128)S(1)} %get-tuple-element.38), channel_id=1, source_target_pairs={{0,28},{4,0},{8,4},{12,8},{16,12},{20,16},{24,20},{28,24},{1,29},{... | collective-permute-start | bytes 147464 | tf_op jit(solution)/shard_map/ppermute | solution.py:460
  31.4 10.9 %all-to-all-start.1 = ((f32[32,1,128]{2,1,0:T(1,128)}), f32[32,1,128]{2,1,0:T(1,128)S(1)}, u32[]{:S(2)}, u32[]{:S(2)}) async-start(f32[32,1,128]{2,1,0:T(1,128)} %bitcast.1), calls=%async_computation.1 | async-start | bytes 32768 | tf_op jit(solution)/shard_map/all_to_all | solution.py:516
  46.0 5.7 %collective-permute-start.7 = (f32[24,8,128]{2,1,0:T(8,128)S(1)}, f32[24,8,128]{2,1,0:T(8,128)S(1)}, u32[]{:S(2)}, u32[]{:S(2)}) collective-permute-start(f32[24,8,128]{2,1,0:T(8,128)S(1)} %get-tuple-element.41), channel_id=1, source_target_pairs={{0,1},{1,0},{2,3},{3,2},{4,5},{5,4},{6,7},{7,6},{8,9},{9,8},{10,11... | collective-permute-start | bytes 294920 | tf_op jit(solution)/shard_map/ppermute | solution.py:465
  46.5 10.5 %collective-permute-start.8 = (f32[24,8,128]{2,1,0:T(8,128)S(1)}, f32[24,8,128]{2,1,0:T(8,128)S(1)}, u32[]{:S(2)}, u32[]{:S(2)}) collective-permute-start(f32[24,8,128]{2,1,0:T(8,128)S(1)} %get-tuple-element.42), channel_id=1, source_target_pairs={{0,2},{1,3},{2,0},{3,1},{4,6},{5,7},{6,4},{7,5},{8,10},{9,11},{10,... | collective-permute-start | bytes 294920 | tf_op jit(solution)/shard_map/ppermute | solution.py:465
  47.1 9.8 %collective-permute-start.9 = (f32[24,8,128]{2,1,0:T(8,128)S(1)}, f32[24,8,128]{2,1,0:T(8,128)S(1)}, u32[]{:S(2)}, u32[]{:S(2)}) collective-permute-start(f32[24,8,128]{2,1,0:T(8,128)S(1)} %get-tuple-element.43), channel_id=1, source_target_pairs={{0,3},{1,2},{2,1},{3,0},{4,7},{5,6},{6,5},{7,4},{8,11},{9,10},{10,... | collective-permute-start | bytes 294920 | tf_op jit(solution)/shard_map/ppermute | solution.py:465
